TPU v7x, 512 devices: a whole 4x4x16 slice. The times are simulated.
512 devices in a mesh: dp: 64 (over y, z_hi, x, core), fsdp: 8 (over z_lo).
Axes of the slice: x: 4, y: 4, z: 16 (z_hi: 2, z_lo: 8; z = z_hi * 8 + z_lo), core: 2. Of those that a mesh axis runs over, the one named last changes fastest.
Arguments:
- inputs: bfloat16 [65536, 4096], P(('dp', 'fsdp')), may hold values from -6 to 6
- out_grad: bfloat16 [65536, 2048], P(('dp', 'fsdp')), may hold values from -24 to 24
- weight: bfloat16 [4096, 2048], P('fsdp'), may hold values from -0.125 to 0.125
- proj_basis: bfloat16 [4096, 256], P('fsdp'), may hold values from -0.09375 to 0.09375
- first_moment: float32 [64, 8192], P('dp'), may hold values from -6 to 6
- second_moment: float32 [64, 8192], P('dp'), may hold values from 0.25 to 4
Outputs:
- input_grad: bfloat16 [65536, 4096], P(('dp', 'fsdp'))
- new_first: float32 [64, 8192], P('dp')
- new_second: float32 [64, 8192], P('dp')
- update: float32 [4096, 2048], P('fsdp', 'dp')
All inputs are finite; a program needn't handle non-finite values.
Results may differ from a plain program's by a relative error of at most 0.0029.
Values may be sent and summed in bfloat16 or wider, within the bound.
No kernel may reach another device: no remote copies, remote signals or barrier semaphores. Data moves between devices by JAX's collectives and lax.ppermute only.
A program may use at most 64 MiB of HBM per device.

v0:
```python
import math
import jax
import jax.numpy as jnp
from jax import lax
from jax.sharding import PartitionSpec as P

STEP = 1000
beta_one = 0.9
beta_two = 0.999
epsilon = 1e-08


def on_device(inputs, out_grad, weight, proj_basis, first_moment, second_moment):
    tok_rows = inputs.shape[0]
    data_count = lax.axis_size("dp")
    shard_count = lax.axis_size("fsdp")
    rank_cols = proj_basis.shape[1]
    feature_grad = lax.dot_general(
        lax.all_gather(out_grad, "fsdp", axis=0, tiled=True),
        weight,
        (((1,), (1,)), ((), ())),
        preferred_element_type=jnp.float32,
    ).astype(jnp.bfloat16)
    input_grad = lax.all_to_all(feature_grad, "fsdp", split_axis=0, concat_axis=1, tiled=True)
    proj_full = jnp.dot(
        inputs,
        lax.all_gather(proj_basis, "fsdp", axis=0, tiled=True),
        preferred_element_type=jnp.float32,
    )
    projected_in = proj_full.astype(jnp.bfloat16)
    scale_factor = 1.0 / math.sqrt(tok_rows * data_count * shard_count)
    low_rank = (
        lax.dot_general(
            projected_in, out_grad, (((0,), (0,)), ((), ())), preferred_element_type=jnp.float32
        )
        * scale_factor
    )
    col_width = low_rank.shape[1] // data_count
    summed = lax.psum(low_rank, ("dp", "fsdp"))
    grad_block = lax.dynamic_slice_in_dim(summed, lax.axis_index("dp") * col_width, col_width, 1)
    flat_grad = grad_block.reshape(1, rank_cols * col_width)
    new_first = beta_one * first_moment + (1.0 - beta_one) * flat_grad
    new_second = beta_two * second_moment + (1.0 - beta_two) * flat_grad * flat_grad
    corr_one = 1.0 - beta_one**STEP
    corr_two = 1.0 - beta_two**STEP
    direction = (new_first / corr_one / (jnp.sqrt(new_second / corr_two) + epsilon)).astype(
        jnp.bfloat16
    )
    direction = direction.reshape(rank_cols, col_width)
    update = jnp.dot(proj_basis, direction, preferred_element_type=jnp.float32)
    return (input_grad, new_first, new_second, update)


def solution(mesh):
    in_specs = (
        P(("dp", "fsdp"), None),
        P(("dp", "fsdp"), None),
        P("fsdp", None),
        P("fsdp", None),
        P("dp", None),
        P("dp", None),
    )
    out_specs = (P(("dp", "fsdp"), None), P("dp", None), P("dp", None), P("fsdp", "dp"))
    return jax.shard_map(
        on_device, mesh=mesh, in_specs=in_specs, out_specs=out_specs, check_vma=False
    )
```

profile of v0, /device:TPU:1, one launch (start us, length us, event | category | flops | bytes accessed | tf_op | source)
XLA Modules:
  0.0 714.3 jit_solution(5845049301039747095)
XLA Ops:
  7.2 0.0 copy-start
  7.2 0.0 all-gather.3.cloned.1.call-start
  7.2 0.7 all-gather.3.cloned.1.call-update
  7.9 0.0 all-gather.5.cloned.1.call-start
  8.0 0.7 all-gather.5.cloned.1.call-update
  8.7 111.0 %all-gather.3.cloned.1.call-done = bf16[1024,2048]{1,0:T(8,128)(2,1)} async-done(((bf16[128,2048]{1,0:T(8,128)(2,1)}), bf16[1024,2048]{1,0:T(8,128)(2,1)}) %all-gather.3.cloned.1.call-update) | async-done | bytes 4194320 | tf_op jit(solution)/shard_map/all_gather | solution.py:19
  119.7 0.0 copy-done
  119.7 5.5 convolution_convert_fusion
  125.2 3.6 all-to-all-start
  128.8 0.0 all-reduce.2.cloned.1.call-start
  128.8 89.4 %all-gather.5.cloned.1.call-done = bf16[4096,256]{1,0:T(8,128)(2,1)} async-done(((bf16[512,256]{1,0:T(8,128)(2,1)}), bf16[4096,256]{1,0:T(8,128)(2,1)}) %all-gather.5.cloned.1.call-update) | async-done | bytes 2097168 | tf_op jit(solution)/shard_map/all_gather | solution.py:27
  218.2 4.7 convolution_multiply_fusion
  222.9 0.0 copy-start.1
  222.9 0.0 all-reduce.2.cloned.1.call-update
  222.9 478.2 %all-reduce.2.cloned.1.call-done = f32[256,2048]{0,1:T(8,128)} async-done(((f32[256,2048]{0,1:T(8,128)}), f32[256,2048]{0,1:T(8,128)}) %all-reduce.2.cloned.1.call-update) | async-done | bytes 2097168 | tf_op jit(solution)/shard_map/psum | solution.py:39
  701.2 1.4 constant_dynamic-slice_fusion
  702.5 0.9 copy.12
  703.4 0.7 reshape.53
  704.1 1.6 convert_reduce_fusion
  705.7 0.1 reshape.54
  705.8 0.0 copy-done.1
  705.8 0.8 convolution_bitcast_fusion
  706.7 0.0 all-to-all-done
  706.7 1.1 copy.13
Async XLA Ops:
  7.2 112.5 %copy-start = (bf16[512,2048]{1,0:T(8,128)(2,1)S(1)}, bf16[512,2048]{1,0:T(8,128)(2,1)}, u32[]{:S(2)}) copy-start(bf16[512,2048]{1,0:T(8,128)(2,1)} %param.8) | copy-start | bytes 6291460
  7.2 112.5 %all-gather.3.cloned.1.call-start = ((), (), s32[]{:S(2)}) async-start(), calls=%async_computation.1 | async-start | bytes 4718592 | tf_op jit(solution)/shard_map/all_gather | solution.py:19
  7.9 210.3 %all-gather.5.cloned.1.call-start = ((), (), s32[]{:S(2)}) async-start(), calls=%async_computation.2 | async-start | bytes 2359296 | tf_op jit(solution)/shard_map/all_gather | solution.py:27
  125.2 581.5 %all-to-all-start = ((bf16[8,128,512]{2,1,0:T(8,128)(2,1)}), bf16[8,128,512]{2,1,0:T(8,128)(2,1)S(1)}, u32[]{:S(2)}, u32[]{:S(2)}) async-start(bf16[8,128,512]{2,1,0:T(8,128)(2,1)} %bitcast.14), calls=%async_computation | async-start | bytes 2097152 | tf_op jit(solution)/shard_map/all_to_all | solution.py:24
  128.8 572.4 %all-reduce.2.cloned.1.call-start = ((), (), s32[]{:S(2)}) async-start(), calls=%async_computation.3 | async-start | bytes 4194304 | tf_op jit(solution)/shard_map/psum | solution.py:39
  222.9 482.9 %copy-start.1 = (bf16[512,256]{1,0:T(8,128)(2,1)S(1)}, bf16[512,256]{1,0:T(8,128)(2,1)}, u32[]{:S(2)}) copy-start(bf16[512,256]{1,0:T(8,128)(2,1)} %param.9) | copy-start | bytes 786436
Sparse Core Ops, SparseCore 0:
  10.1 109.5 all-gather.2
  121.8 96.4 all-gather.4
  223.6 477.5 all-reduce.1
where the time goes:
time: 715 us; the launch traced here: 714 us
  waiting for transfers between devices  680 us (95%)
  between operations  13.8 us (2%)
  matrix products  11 us (2%)
    psum x1, waiting for transfers between devices, on_device(): summed = lax.psum(low_rank, ('dp', 'fsdp'))  478 us
    all_gather x1, waiting for transfers between devices, on_device(): lax.all_gather(out_grad, 'fsdp', axis=0, tiled=True)  111 us
    all_gather x1, waiting for transfers between devices, on_device(): lax.all_gather(proj_basis, 'fsdp', axis=0, tiled=True)  89.4 us
  transfers between devices with their start and end apart: 4, of which 3 were waited for; matrix products, arithmetic and copies ran while one was open for 2% of the time, Pallas kernels for 0%

commit v1 on v0

--- a/solution.py
+++ b/solution.py
@@ -3,6 +3,7 @@
 import jax.numpy as jnp
 from jax import lax
 from jax.sharding import PartitionSpec as P
+from jax.lax import psum
 
 STEP = 1000
 beta_one = 0.9
@@ -36,7 +37,9 @@
         * scale_factor
     )
     col_width = low_rank.shape[1] // data_count
-    summed = lax.psum(low_rank, ("dp", "fsdp"))
+    summed = low_rank
+    for dd in ("fsdp", "dp"):
+        summed = psum(summed, dd)
     grad_block = lax.dynamic_slice_in_dim(summed, lax.axis_index("dp") * col_width, col_width, 1)
     flat_grad = grad_block.reshape(1, rank_cols * col_width)
     new_first = beta_one * first_moment + (1.0 - beta_one) * flat_grad

time: 715 us -> 1450 us (2.03)
  waiting for transfers between devices: 680 us -> 1420 us
    psum x1 -> x2, waiting for transfers between devices: 478 us -> 1240 us  [on_device(): summed = psum(summed, dd)]
    all_gather x1, waiting for transfers between devices: 89.4 us -> 72.6 us  [on_device(): lax.all_gather(proj_basis, 'fsdp', axis=0, tiled=True)]
  transfers between devices with their start and end apart: 4 -> 5, of which waited for: 3 -> 4; matrix products, arithmetic and copies ran while one was open for 2% -> 1% of each run, Pallas kernels for 0% -> 0%
where the time goes in v1:
time: 1450 us
  waiting for transfers between devices  1420 us (98%)
    psum x2, waiting for transfers between devices, on_device(): summed = psum(summed, dd)  1240 us
    all_gather x1, waiting for transfers between devices, on_device(): lax.all_gather(out_grad, 'fsdp', axis=0, tiled=True)  103 us
    all_gather x1, waiting for transfers between devices, on_device(): lax.all_gather(proj_basis, 'fsdp', axis=0, tiled=True)  72.6 us
  transfers between devices with their start and end apart: 5, of which 4 were waited for; matrix products, arithmetic and copies ran while one was open for 1% of the time, Pallas kernels for 0%

profile of v1, /device:TPU:1, one launch (start us, length us, event | category | flops | bytes accessed | tf_op | source)
XLA Modules:
  0.0 1453.4 jit_solution(15406085166230876925)
XLA Ops:
  7.2 0.0 copy-start
  7.2 0.0 all-gather.5.cloned.1.call-start
  7.2 0.7 all-gather.5.cloned.1.call-update
  7.9 0.0 all-gather.3.cloned.1.call-start
  8.0 0.7 all-gather.3.cloned.1.call-update
  8.7 0.0 all-reduce.3.cloned.1.call-start
  8.7 72.6 %all-gather.5.cloned.1.call-done = bf16[4096,256]{1,0:T(8,128)(2,1)} async-done(((bf16[512,256]{1,0:T(8,128)(2,1)}), bf16[4096,256]{1,0:T(8,128)(2,1)}) %all-gather.5.cloned.1.call-update) | async-done | bytes 2097168 | tf_op jit(solution)/shard_map/all_gather | solution.py:28
  81.3 4.7 convolution_multiply_fusion
  86.0 0.0 all-reduce.3.cloned.1.call-update
  86.0 102.5 %all-gather.3.cloned.1.call-done = bf16[1024,2048]{1,0:T(8,128)(2,1)} async-done(((bf16[128,2048]{1,0:T(8,128)(2,1)}), bf16[1024,2048]{1,0:T(8,128)(2,1)}) %all-gather.3.cloned.1.call-update) | async-done | bytes 4194320 | tf_op jit(solution)/shard_map/all_gather | solution.py:20
  188.5 5.5 convolution_convert_fusion
  194.0 3.7 all-to-all-start
  197.7 0.0 all-reduce.5.cloned.1.call-start
  197.8 157.3 %all-reduce.3.cloned.1.call-done = f32[256,2048]{0,1:T(8,128)} async-done(((f32[256,2048]{0,1:T(8,128)}), f32[256,2048]{0,1:T(8,128)}) %all-reduce.3.cloned.1.call-update) | async-done | bytes 2097168 | tf_op jit(solution)/shard_map/psum | solution.py:42
  355.1 0.0 all-reduce.5.cloned.1.call-update
  355.1 1085.2 %all-reduce.5.cloned.1.call-done = f32[256,2048]{0,1:T(8,128)} async-done(((f32[256,2048]{0,1:T(8,128)}), f32[256,2048]{0,1:T(8,128)}) %all-reduce.5.cloned.1.call-update) | async-done | bytes 2097168 | tf_op jit(solution)/shard_map/psum | solution.py:42
  1440.3 1.4 constant_dynamic-slice_fusion
  1441.7 0.9 copy.12
  1442.6 0.7 reshape.53
  1443.3 1.6 convert_reduce_fusion
  1444.9 0.1 reshape.54
  1445.0 0.8 convolution_bitcast_fusion
  1445.8 0.0 all-to-all-done
  1445.8 1.1 copy.13
  (3 shorter events, 0.0 us)
Async XLA Ops:
  7.2 181.3 %copy-start = (bf16[512,2048]{1,0:T(8,128)(2,1)S(1)}, bf16[512,2048]{1,0:T(8,128)(2,1)}, u32[]{:S(2)}) copy-start(bf16[512,2048]{1,0:T(8,128)(2,1)} %param.8) | copy-start | bytes 6291460
  7.2 74.1 %all-gather.5.cloned.1.call-start = ((), (), s32[]{:S(2)}) async-start(), calls=%async_computation.2 | async-start | bytes 2359296 | tf_op jit(solution)/shard_map/all_gather | solution.py:28
  7.9 180.6 %all-gather.3.cloned.1.call-start = ((), (), s32[]{:S(2)}) async-start(), calls=%async_computation.1 | async-start | bytes 4718592 | tf_op jit(solution)/shard_map/all_gather | solution.py:20
  8.7 346.4 %all-reduce.3.cloned.1.call-start = ((), (), s32[]{:S(2)}) async-start(), calls=%async_computation.3 | async-start | bytes 4194304 | tf_op jit(solution)/shard_map/psum | solution.py:42
  194.0 1251.0 %copy-start.1 = (bf16[512,256]{1,0:T(8,128)(2,1)S(1)}, bf16[512,256]{1,0:T(8,128)(2,1)}, u32[]{:S(2)}) copy-start(bf16[512,256]{1,0:T(8,128)(2,1)} %param.9) | copy-start | bytes 786436
  194.0 1251.8 %all-to-all-start = ((bf16[8,128,512]{2,1,0:T(8,128)(2,1)}), bf16[8,128,512]{2,1,0:T(8,128)(2,1)S(1)}, u32[]{:S(2)}, u32[]{:S(2)}) async-start(bf16[8,128,512]{2,1,0:T(8,128)(2,1)} %bitcast.14), calls=%async_computation | async-start | bytes 2097152 | tf_op jit(solution)/shard_map/all_to_all | solution.py:25
  197.7 1242.6 %all-reduce.5.cloned.1.call-start = ((), (), s32[]{:S(2)}) async-start(), calls=%async_computation.4 | async-start | bytes 4194304 | tf_op jit(solution)/shard_map/psum | solution.py:42
Sparse Core Ops, SparseCore 0:
  10.1 71.1 all-gather.4
  83.3 105.0 all-gather.2
  191.4 163.6 all-reduce.2
  357.9 1082.4 all-reduce.4
